TPU v7x, 256 devices: a whole 4x4x8 slice. The times are simulated.
256 devices in a mesh: seq: 32 (over z, y), mp: 8 (over x, core).
Axes of the slice: x: 4, y: 4, z: 8, core: 2. Of those that a mesh axis runs over, the one named last changes fastest.
Arguments:
- scored_token_targets: int32 [8192], P('seq'), may hold values from 0 to 15999
- valid: int32 [8192], P('seq'), may hold values 0 or 1
- lengths: int32 [48], replicated, may hold values from 1 to 1024, 8192 in all
- owners: int32 [48], replicated, may hold values from 0 to 31
- holders: int32 [48], replicated, may hold values from -1 to 31, as said below
- mixer_input_x: bfloat16 [2, 8192, 3584], P(None, 'seq', 'mp'), may hold values from -6 to 6
- mixer_gate_input: bfloat16 [2, 8192, 3584], P(None, 'seq', 'mp'), may hold values from -6 to 6
- input_projection_b: bfloat16 [2, 8192, 64], P(None, 'seq'), may hold values from -2.390625 to 2.390625
- output_projection_c: bfloat16 [2, 8192, 64], P(None, 'seq'), may hold values from -2.390625 to 2.390625
- token_step_sizes: float32 [2, 8192, 56], P(None, 'seq', 'mp'), may hold values from 0.01 to 0.3
- head_decay_rate: float32 [2, 56], P(None, 'mp'), may hold values from 0.0002 to 1
- head_skip_scale: float32 [2, 56], P(None, 'mp'), may hold values from 0.5 to 1.5
- prompt_held_states: bfloat16 [2, 32, 56, 64, 64], P(None, 'seq', 'mp'), may hold values from -6 to 6
- shared_output_weight: bfloat16 [3584, 3584], P('mp'), may hold values from -0.09375 to 0.09375
- adapter_down_weight: bfloat16 [3584, 128], P('mp'), may hold values from -0.09375 to 0.09375
- adapter_up_weight: bfloat16 [128, 3584], replicated, may hold values from -0.5 to 0.5
- residual: bfloat16 [8192, 2, 3584], P('seq'), may hold values from -16 to 16
- final_norm_scale: float32 [3584], replicated, may hold values from 0.5 to 1.5
- vocab_head_weight: bfloat16 [3584, 16000], P('seq', 'mp'), may hold values from -8 to 8
Outputs:
- owner_sums: float32 [32, 48], P('seq')
- token_delta: float32 [8192], P('seq')
Inputs may be any that keep to these rules, and one draw needn't show every extreme that they name: `holders`: exactly 24 rollouts continue a prompt state; the others start from zeros.
All inputs are finite; a program needn't handle non-finite values. No bound on the sum of `valid` on one device may be relied on, other than what follows from the above.
Results may differ from a plain program's by a relative error of at most 0.035.
Values may be sent and summed in bfloat16 or wider, within the bound.
A program may use at most 128 MiB of HBM per device.

v0:
```python
import jax
import jax.numpy as jnp
from jax import lax
from jax.sharding import PartitionSpec as P

highest = lax.Precision.HIGHEST


def shifted(x, axis, by):
    count = lax.axis_size(axis)
    pairs = [(i, i + by) for i in range(count) if 0 <= i + by < count]
    return lax.ppermute(x, axis, pairs)


def root_norm(hidden, final_norm_scale):
    mean_sq = jnp.mean(hidden * hidden, axis=-1, keepdims=True)
    return (hidden * lax.rsqrt(mean_sq + 1e-05) * final_norm_scale).astype(jnp.bfloat16)


def shards(
    scored_token_targets,
    valid,
    lengths,
    owners,
    holders,
    mixer_input_x,
    mixer_gate_input,
    input_projection_b,
    output_projection_c,
    token_step_sizes,
    head_decay_rate,
    head_skip_scale,
    prompt_held_states,
    shared_output_weight,
    adapter_down_weight,
    adapter_up_weight,
    residual,
    final_norm_scale,
    vocab_head_weight,
):
    seq_count = lax.axis_size("seq")
    mp_count = lax.axis_size("mp")
    tok_rows = scored_token_targets.shape[0]
    models = mixer_input_x.shape[0]
    inner_local = mixer_input_x.shape[2]
    head_count = token_step_sizes.shape[2]
    head_dim = inner_local // head_count
    state_dim = input_projection_b.shape[2]
    roll_count = lengths.shape[0]
    first_row = lax.axis_index("seq") * tok_rows
    offsets = jnp.arange(tok_rows, dtype=jnp.int32)
    position = first_row + offsets
    starts = jnp.cumsum(lengths) - lengths
    rollout = jnp.sum((starts[None, :] <= position[:, None]).astype(jnp.int32), axis=1) - 1
    member_table = rollout[:, None] == jnp.arange(roll_count, dtype=jnp.int32)[None, :]
    start_local = jnp.sum(jnp.where(member_table, starts[None, :], 0), axis=1) - first_row
    holder_tok = jnp.sum(jnp.where(member_table, holders[None, :], 0), axis=1)
    borrowed = (start_local >= 0) & (holder_tok >= 0)
    prompt_pick = (
        (holder_tok[:, None] == jnp.arange(seq_count, dtype=jnp.int32)[None, :]) & borrowed[:, None]
    ).astype(jnp.float32)
    neg_rates = -head_decay_rate
    log_decay = jnp.cumsum(token_step_sizes * neg_rates[:, None, :], axis=1)
    before = jnp.take(log_decay, jnp.maximum(start_local - 1, 0), axis=1)
    before = jnp.where((start_local >= 1)[None, :, None], before, 0.0)
    x_values = mixer_input_x.astype(jnp.float32).reshape(models, tok_rows, head_count, head_dim)
    b_values = input_projection_b.astype(jnp.float32)
    c_values = output_projection_c.astype(jnp.float32)
    gram_matrix = jnp.einsum(
        "mtn,msn->mts", output_projection_c, input_projection_b, preferred_element_type=jnp.float32
    )
    causal = (rollout[:, None] == rollout[None, :]) & (offsets[None, :] <= offsets[:, None])
    log_gap = log_decay[:, :, None, :] - log_decay[:, None, :, :]
    mixing = jnp.where(
        causal[None, :, :, None], jnp.exp(jnp.where(causal[None, :, :, None], log_gap, 0.0)), 0.0
    )
    mixing = mixing * gram_matrix[..., None] * token_step_sizes[:, None, :, :]
    intra_out = jnp.einsum("mtsh,mshp->mthp", mixing, x_values, precision=highest)
    last_pick = prompt_pick[tok_rows - 1]
    zeros_state = jnp.zeros((models, head_count, head_dim, state_dim), jnp.float32)
    piece = lax.all_gather(prompt_held_states, "seq", axis=1, tiled=True)
    last_weight = last_pick.astype(jnp.bfloat16)
    picked = (prompt_pick[None, :, :, None] * c_values[:, :, None, :]).astype(jnp.bfloat16)
    projected = jnp.einsum("mtjn,mjhpn->mthp", picked, piece, preferred_element_type=jnp.float32)
    end_states = jnp.einsum("j,mjhpn->mhpn", last_weight, piece, preferred_element_type=jnp.float32)
    entry_decay = jnp.exp(log_decay - before)
    final_log = log_decay[:, tok_rows - 1, :]
    tail_mask = (rollout == rollout[tok_rows - 1]).astype(jnp.float32)
    end_weight = (
        jnp.exp(final_log[:, None, :] - log_decay) * token_step_sizes * tail_mask[None, :, None]
    )
    local_end = jnp.einsum("msh,mshp,msn->mhpn", end_weight, x_values, b_values, precision=highest)
    local_end = (
        local_end + jnp.exp(final_log - before[:, tok_rows - 1, :])[:, :, None, None] * end_states
    )
    carry_through = jnp.where(start_local[tok_rows - 1] < 0, jnp.exp(final_log), 0.0)

    def relay_step(step_index, incoming):
        outgoing = carry_through[:, :, None, None] * incoming + local_end
        return shifted(outgoing, "seq", 1)

    arriving = lax.fori_loop(0, seq_count - 1, relay_step, zeros_state)
    inherited = (start_local < 0).astype(jnp.float32)
    carried = jnp.einsum("mhpn,mtn->mthp", arriving, c_values, precision=highest)
    carried = carried * (jnp.exp(log_decay) * inherited[None, :, None])[..., None]
    output = (
        intra_out
        + carried
        + entry_decay[..., None] * projected
        + head_skip_scale[:, None, :, None] * x_values
    )
    output = output.reshape(models, tok_rows, inner_local)
    gated_output = (output * jax.nn.silu(mixer_gate_input.astype(jnp.float32))).astype(jnp.bfloat16)
    share_rows = tok_rows // mp_count
    base_output = jnp.einsum(
        "mti,id->tmd", gated_output, shared_output_weight, preferred_element_type=jnp.float32
    )
    low_rank_rows = jnp.dot(
        gated_output[0], adapter_down_weight, preferred_element_type=jnp.float32
    ).astype(jnp.bfloat16)
    adapter_output = jnp.dot(low_rank_rows, adapter_up_weight, preferred_element_type=jnp.float32)
    mixed = lax.psum_scatter(
        jnp.stack([base_output[:, 0] + adapter_output, base_output[:, 1]], axis=1).astype(
            jnp.bfloat16
        ),
        "mp",
        scatter_dimension=0,
        tiled=True,
    ).astype(jnp.float32)
    own_rows = lax.dynamic_slice_in_dim(residual, lax.axis_index("mp") * share_rows, share_rows, 0)
    normed_own = root_norm(own_rows.astype(jnp.float32) + mixed, final_norm_scale)
    normed = lax.all_gather(normed_own, "mp", axis=0, tiled=True)
    vocab_local = vocab_head_weight.shape[1]
    logits = jnp.einsum(
        "tmk,kv->mtv",
        normed,
        lax.all_gather(vocab_head_weight, "seq", axis=0, tiled=True),
        preferred_element_type=jnp.float32,
    )
    vocab_first = lax.axis_index("mp") * vocab_local
    target_hit = (
        scored_token_targets[:, None]
        == vocab_first + jnp.arange(vocab_local, dtype=jnp.int32)[None, :]
    )
    target_local = jnp.sum(jnp.where(target_hit[None], logits, 0.0), axis=2)
    local_max = jnp.max(logits, axis=2)
    vocab_top = lax.pmax(local_max, "mp")
    exp_sums = jnp.sum(jnp.exp(logits - vocab_top[..., None]), axis=2)
    vocab_total, target_logit = lax.psum((exp_sums, target_local), "mp")
    logprob = target_logit - vocab_top - jnp.log(vocab_total)
    token_delta = (logprob[0] - logprob[1]) * valid.astype(jnp.float32)
    roll_sums = jnp.dot(
        token_delta, member_table.astype(jnp.float32), precision=highest
    ) / lengths.astype(jnp.float32)
    owner_rows = (owners[None, :] == jnp.arange(seq_count, dtype=jnp.int32)[:, None]).astype(
        jnp.float32
    ) * roll_sums[None, :]
    owner_sums = lax.psum_scatter(owner_rows, "seq", scatter_dimension=0, tiled=True)
    return (owner_sums, token_delta)


def solution(mesh):
    placed = (
        P("seq"),
        P("seq"),
        P(),
        P(),
        P(),
        P(None, "seq", "mp"),
        P(None, "seq", "mp"),
        P(None, "seq", None),
        P(None, "seq", None),
        P(None, "seq", "mp"),
        P(None, "mp"),
        P(None, "mp"),
        P(None, "seq", "mp", None, None),
        P("mp", None),
        P("mp", None),
        P(),
        P("seq", None, None),
        P(),
        P("seq", "mp"),
    )
    return jax.shard_map(
        shards, mesh=mesh, in_specs=placed, out_specs=(P("seq", None), P("seq")), check_vma=False
    )
```

profile of v0, /device:TPU:0, one launch (start us, length us, event | category | flops | bytes accessed | tf_op | source)
XLA Modules:
  0.0 1076.7 jit_solution(12704770804620089405)
XLA Ops:
  35.8 69.4 %all-gather.4.cloned.1.call-done = bf16[2,32,7,64,64]{4,3,1,2,0:T(8,128)(2,1)} async-done(((bf16[2,1,7,64,64]{4,3,1,2,0:T(8,128)(2,1)}), bf16[2,32,7,64,64]{4,3,1,2,0:T(8,128)(2,1)}) %all-gather.4.cloned.1.call-update) | async-done | bytes 3670032 | tf_op jit(solution)/shard_map/all_gather | solution.py:81
  105.2 7.4 fusion.2
  117.8 498.9 %while.10 = (s32[]{:T(128)}, f32[2,7,64,64]{3,2,1,0:T(8,128)}, f32[2,7]{1,0:T(2,128)S(1)}, f32[2,7,64,64]{3,2,1,0:T(8,128)}, s32[]{:T(128)}) while((s32[]{:T(128)}, f32[2,7,64,64]{3,2,1,0:T(8,128)}, f32[2,7]{1,0:T(2,128)S(1)}, f32[2,7,64,64]{3,2,1,0:T(8,128)}, s32[]{:T(128)}) %tuple.33), condition=%wide.region_7.8_spmd, body=%wide.region_6.7_spmd.sunk | while | flops 114690 | bytes 1605789 | solution.py:102
  122.8 8.9 collective-permute-done
  138.9 7.9 collective-permute-done
  154.1 7.0 collective-permute-done
  168.3 6.1 collective-permute-done
  181.6 5.5 collective-permute-done
  194.4 5.5 collective-permute-done
  201.9 5.9 collective-permute-start
  207.8 5.5 collective-permute-done
  215.3 7.3 collective-permute-start
  222.6 5.5 collective-permute-done
  230.1 7.5 collective-permute-start
  237.6 6.4 collective-permute-done
  246.1 7.9 collective-permute-start
  254.0 7.5 collective-permute-done
  263.5 8.2 collective-permute-start
  271.7 8.6 collective-permute-done
  282.3 8.2 collective-permute-start
  290.5 9.8 collective-permute-done
  302.4 8.2 collective-permute-start
  310.6 9.9 collective-permute-done
  322.5 7.6 collective-permute-start
  330.1 8.7 collective-permute-done
  340.8 6.4 collective-permute-start
  347.2 7.4 collective-permute-done
  356.7 7.3 collective-permute-start
  364.0 6.5 collective-permute-done
  372.5 7.3 collective-permute-start
  379.8 5.6 collective-permute-done
  387.4 7.3 collective-permute-start
  394.7 5.5 collective-permute-done
  402.3 7.3 collective-permute-start
  417.1 7.3 collective-permute-start
  431.9 7.3 collective-permute-start
  439.2 5.5 collective-permute-done
  446.8 7.3 collective-permute-start
  454.1 6.1 collective-permute-done
  462.2 7.6 collective-permute-start
  469.8 7.1 collective-permute-done
  479.0 8.2 collective-permute-start
  487.1 8.2 collective-permute-done
  497.4 8.2 collective-permute-start
  505.6 9.3 collective-permute-done
  517.0 8.2 collective-permute-start
  525.2 10.3 collective-permute-done
  537.5 7.6 collective-permute-start
  545.1 9.1 collective-permute-done
  556.3 7.1 collective-permute-start
  563.4 8.0 collective-permute-done
  573.4 6.8 collective-permute-start
  580.2 6.9 collective-permute-done
  589.1 7.3 collective-permute-start
  596.4 5.5 collective-permute-done
  603.9 7.3 collective-permute-start
  611.2 5.5 collective-permute-done
  637.7 81.4 %reduce-scatter.2.cloned.1.call-done = bf16[32,2,3584]{2,0,1:T(8,128)(2,1)} async-done(((bf16[256,2,3584]{2,0,1:T(8,128)(2,1)}), bf16[32,2,3584]{2,0,1:T(8,128)(2,1)}) %reduce-scatter.2.cloned.1.call-update) | async-done | bytes 458768 | tf_op jit(solution)/shard_map/reduce_scatter | solution.py:122
  725.5 28.5 %all-gather.6.cloned.1.call-done = bf16[256,2,3584]{2,0,1:T(8,128)(2,1)} async-done(((bf16[32,2,3584]{2,0,1:T(8,128)(2,1)}), bf16[256,2,3584]{2,0,1:T(8,128)(2,1)}) %all-gather.6.cloned.1.call-update) | async-done | bytes 3670032 | tf_op jit(solution)/shard_map/all_gather | solution.py:132
  753.9 132.5 %all-gather.8.cloned.1.call-done = bf16[3584,2000]{1,0:T(8,128)(2,1)} async-done(((bf16[112,2000]{1,0:T(8,128)(2,1)}), bf16[3584,2000]{1,0:T(8,128)(2,1)}) %all-gather.8.cloned.1.call-update) | async-done | bytes 14336016 | tf_op jit(solution)/shard_map/all_gather | solution.py:137
  886.4 13.6 %fusion.6 = (f32[2,256]{1,0:T(2,128)S(1)}, f32[2,256]{1,0:T(2,128)S(1)}, f32[256,2,2000]{0,2,1:T(8,128)}) fusion(pred[256,2000]{0,1:T(8,128)(4,1)} %broadcast_compare_fusion, bf16[256,2,3584]{2,0,1:T(8,128)(2,1)} %all-gather.6.cloned.1.call-done, bf16[3584,2000]{1,0:T(8,128)(2,1)} %all-gather.8.cloned.1.call-done), kind=kOutput, calls=%fused_computation.14 | convolution fusion | flops 7343102976 | bytes 22618112 | tf_op jit(solution)/shard_map/tmk,kv->mtv/dot_general | solution.py:134
  900.0 14.3 %pmax.7 = f32[2,256]{1,0:T(2,128)S(1)} all-reduce(f32[2,256]{1,0:T(2,128)S(1)} %get-tuple-element.26), channel_id=1, replica_groups=mesh['seq'=32,'mp'=8] {'mp'}, use_global_device_ids=true, to_apply=%region_13.14 | all-reduce | flops 512 | bytes 4096 | tf_op jit(solution)/shard_map/pmax | solution.py:147
  917.1 12.4 %all-reduce.1 = (f32[2,256]{1,0:T(2,128)S(1)}, f32[2,256]{1,0:T(2,128)S(1)}) all-reduce(f32[2,256]{1,0:T(2,128)S(1)} %fusion.8, f32[2,256]{1,0:T(2,128)S(1)} %get-tuple-element.25), channel_id=1, replica_groups=mesh['seq'=32,'mp'=8] {'mp'}, use_global_device_ids=true, to_apply=%region_15.16 | all-reduce | flops 1024 | bytes 8192 | tf_op jit(solution)/shard_map/psum | solution.py:149
  929.7 139.3 %all-reduce = f32[32,48]{1,0:T(8,128)S(1)} all-reduce(f32[32,48]{1,0:T(8,128)S(1)} %fusion.54), channel_id=3, replica_groups=mesh['seq'=32,'mp'=8] {'seq'}, use_global_device_ids=true, to_apply=%region_16.17.clone | all-reduce | flops 1536 | bytes 12288
  (157 shorter events, 167.6 us)
Async XLA Ops:
  7.2 613.1 %copy-start = (bf16[448,3584]{1,0:T(8,128)(2,1)S(1)}, bf16[448,3584]{1,0:T(8,128)(2,1)}, u32[]{:S(2)}) copy-start(bf16[448,3584]{1,0:T(8,128)(2,1)} %param.34) | copy-start | bytes 9633796
  7.2 98.0 %all-gather.4.cloned.1.call-start = ((), (), s32[]{:S(2)}) async-start(), calls=%async_computation.1 | async-start | bytes 7569408 | tf_op jit(solution)/shard_map/all_gather | solution.py:81
  7.9 711.2 %reduce-scatter.2.cloned.1.call-start = ((), (), s32[]{:S(2)}) async-start(), calls=%async_computation.2 | async-start | bytes 4128768 | tf_op jit(solution)/shard_map/reduce_scatter | solution.py:122
  19.7 4.8 copy-start.11
  30.4 82.1 %copy-start.7 = (bf16[2,256,64]{1,2,0:T(8,128)(2,1)S(1)}, bf16[2,256,64]{1,2,0:T(8,128)(2,1)}, u32[]{:S(2)}) copy-start(bf16[2,256,64]{1,2,0:T(8,128)(2,1)} %param.28) | copy-start | bytes 196612
  105.2 7.4 copy-start.4
  105.2 8.8 copy-start.2
  105.2 8.8 copy-start.10
  117.0 499.8 %copy-start.5 = (bf16[2,256,64]{1,2,0:T(8,128)(2,1)S(1)}, bf16[2,256,64]{1,2,0:T(8,128)(2,1)}, u32[]{:S(2)}) copy-start(bf16[2,256,64]{1,2,0:T(8,128)(2,1)} %param.29) | copy-start | bytes 196612
  117.0 499.8 %copy-start.15 = (f32[2,7]{1,0:T(2,128)S(1)}, f32[2,7]{1,0:T(2,128)}, u32[]{:S(2)}) copy-start(f32[2,7]{1,0:T(2,128)} %param.32) | copy-start | bytes 172
  119.9 11.8 %collective-permute-start = (f32[2,7,64,64]{3,2,1,0:T(8,128)}, f32[2,7,64,64]{3,2,1,0:T(8,128)}, u32[]{:S(2)}, u32[]{:S(2)}) collective-permute-start(f32[2,7,64,64]{3,2,1,0:T(8,128)} %multiply_add_fusion.2), channel_id=1, source_target_pairs={{0,8},{8,16},{16,24},{24,32},{32,40},{40,48},{48,56},{56,64},{64,7... | collective-permute-start | bytes 688136 | tf_op jit(solution)/shard_map/while/body/eval_jaxpr/ppermute | solution.py:12
  133.7 13.1 %collective-permute-start = (f32[2,7,64,64]{3,2,1,0:T(8,128)}, f32[2,7,64,64]{3,2,1,0:T(8,128)}, u32[]{:S(2)}, u32[]{:S(2)}) collective-permute-start(f32[2,7,64,64]{3,2,1,0:T(8,128)} %multiply_add_fusion.2), channel_id=1, source_target_pairs={{0,8},{8,16},{16,24},{24,32},{32,40},{40,48},{48,56},{56,64},{64,7... | collective-permute-start | bytes 688136 | tf_op jit(solution)/shard_map/while/body/eval_jaxpr/ppermute | solution.py:12
  148.9 12.2 %collective-permute-start = (f32[2,7,64,64]{3,2,1,0:T(8,128)}, f32[2,7,64,64]{3,2,1,0:T(8,128)}, u32[]{:S(2)}, u32[]{:S(2)}) collective-permute-start(f32[2,7,64,64]{3,2,1,0:T(8,128)} %multiply_add_fusion.2), channel_id=1, source_target_pairs={{0,8},{8,16},{16,24},{24,32},{32,40},{40,48},{48,56},{56,64},{64,7... | collective-permute-start | bytes 688136 | tf_op jit(solution)/shard_map/while/body/eval_jaxpr/ppermute | solution.py:12
  163.1 11.3 %collective-permute-start = (f32[2,7,64,64]{3,2,1,0:T(8,128)}, f32[2,7,64,64]{3,2,1,0:T(8,128)}, u32[]{:S(2)}, u32[]{:S(2)}) collective-permute-start(f32[2,7,64,64]{3,2,1,0:T(8,128)} %multiply_add_fusion.2), channel_id=1, source_target_pairs={{0,8},{8,16},{16,24},{24,32},{32,40},{40,48},{48,56},{56,64},{64,7... | collective-permute-start | bytes 688136 | tf_op jit(solution)/shard_map/while/body/eval_jaxpr/ppermute | solution.py:12
  176.4 10.7 collective-permute-start
  189.2 10.7 collective-permute-start
  201.9 11.4 %collective-permute-start = (f32[2,7,64,64]{3,2,1,0:T(8,128)}, f32[2,7,64,64]{3,2,1,0:T(8,128)}, u32[]{:S(2)}, u32[]{:S(2)}) collective-permute-start(f32[2,7,64,64]{3,2,1,0:T(8,128)} %multiply_add_fusion.2), channel_id=1, source_target_pairs={{0,8},{8,16},{16,24},{24,32},{32,40},{40,48},{48,56},{56,64},{64,7... | collective-permute-start | bytes 688136 | tf_op jit(solution)/shard_map/while/body/eval_jaxpr/ppermute | solution.py:12
  215.3 12.8 %collective-permute-start = (f32[2,7,64,64]{3,2,1,0:T(8,128)}, f32[2,7,64,64]{3,2,1,0:T(8,128)}, u32[]{:S(2)}, u32[]{:S(2)}) collective-permute-start(f32[2,7,64,64]{3,2,1,0:T(8,128)} %multiply_add_fusion.2), channel_id=1, source_target_pairs={{0,8},{8,16},{16,24},{24,32},{32,40},{40,48},{48,56},{56,64},{64,7... | collective-permute-start | bytes 688136 | tf_op jit(solution)/shard_map/while/body/eval_jaxpr/ppermute | solution.py:12
  230.1 13.9 %collective-permute-start = (f32[2,7,64,64]{3,2,1,0:T(8,128)}, f32[2,7,64,64]{3,2,1,0:T(8,128)}, u32[]{:S(2)}, u32[]{:S(2)}) collective-permute-start(f32[2,7,64,64]{3,2,1,0:T(8,128)} %multiply_add_fusion.2), channel_id=1, source_target_pairs={{0,8},{8,16},{16,24},{24,32},{32,40},{40,48},{48,56},{56,64},{64,7... | collective-permute-start | bytes 688136 | tf_op jit(solution)/shard_map/while/body/eval_jaxpr/ppermute | solution.py:12
  246.1 15.4 %collective-permute-start = (f32[2,7,64,64]{3,2,1,0:T(8,128)}, f32[2,7,64,64]{3,2,1,0:T(8,128)}, u32[]{:S(2)}, u32[]{:S(2)}) collective-permute-start(f32[2,7,64,64]{3,2,1,0:T(8,128)} %multiply_add_fusion.2), channel_id=1, source_target_pairs={{0,8},{8,16},{16,24},{24,32},{32,40},{40,48},{48,56},{56,64},{64,7... | collective-permute-start | bytes 688136 | tf_op jit(solution)/shard_map/while/body/eval_jaxpr/ppermute | solution.py:12
  263.5 16.8 %collective-permute-start = (f32[2,7,64,64]{3,2,1,0:T(8,128)}, f32[2,7,64,64]{3,2,1,0:T(8,128)}, u32[]{:S(2)}, u32[]{:S(2)}) collective-permute-start(f32[2,7,64,64]{3,2,1,0:T(8,128)} %multiply_add_fusion.2), channel_id=1, source_target_pairs={{0,8},{8,16},{16,24},{24,32},{32,40},{40,48},{48,56},{56,64},{64,7... | collective-permute-start | bytes 688136 | tf_op jit(solution)/shard_map/while/body/eval_jaxpr/ppermute | solution.py:12
  282.3 18.0 %collective-permute-start = (f32[2,7,64,64]{3,2,1,0:T(8,128)}, f32[2,7,64,64]{3,2,1,0:T(8,128)}, u32[]{:S(2)}, u32[]{:S(2)}) collective-permute-start(f32[2,7,64,64]{3,2,1,0:T(8,128)} %multiply_add_fusion.2), channel_id=1, source_target_pairs={{0,8},{8,16},{16,24},{24,32},{32,40},{40,48},{48,56},{56,64},{64,7... | collective-permute-start | bytes 688136 | tf_op jit(solution)/shard_map/while/body/eval_jaxpr/ppermute | solution.py:12
  302.4 18.1 %collective-permute-start = (f32[2,7,64,64]{3,2,1,0:T(8,128)}, f32[2,7,64,64]{3,2,1,0:T(8,128)}, u32[]{:S(2)}, u32[]{:S(2)}) collective-permute-start(f32[2,7,64,64]{3,2,1,0:T(8,128)} %multiply_add_fusion.2), channel_id=1, source_target_pairs={{0,8},{8,16},{16,24},{24,32},{32,40},{40,48},{48,56},{56,64},{64,7... | collective-permute-start | bytes 688136 | tf_op jit(solution)/shard_map/while/body/eval_jaxpr/ppermute | solution.py:12
  322.5 16.2 %collective-permute-start = (f32[2,7,64,64]{3,2,1,0:T(8,128)}, f32[2,7,64,64]{3,2,1,0:T(8,128)}, u32[]{:S(2)}, u32[]{:S(2)}) collective-permute-start(f32[2,7,64,64]{3,2,1,0:T(8,128)} %multiply_add_fusion.2), channel_id=1, source_target_pairs={{0,8},{8,16},{16,24},{24,32},{32,40},{40,48},{48,56},{56,64},{64,7... | collective-permute-start | bytes 688136 | tf_op jit(solution)/shard_map/while/body/eval_jaxpr/ppermute | solution.py:12
  340.8 13.8 %collective-permute-start = (f32[2,7,64,64]{3,2,1,0:T(8,128)}, f32[2,7,64,64]{3,2,1,0:T(8,128)}, u32[]{:S(2)}, u32[]{:S(2)}) collective-permute-start(f32[2,7,64,64]{3,2,1,0:T(8,128)} %multiply_add_fusion.2), channel_id=1, source_target_pairs={{0,8},{8,16},{16,24},{24,32},{32,40},{40,48},{48,56},{56,64},{64,7... | collective-permute-start | bytes 688136 | tf_op jit(solution)/shard_map/while/body/eval_jaxpr/ppermute | solution.py:12
  356.7 13.8 %collective-permute-start = (f32[2,7,64,64]{3,2,1,0:T(8,128)}, f32[2,7,64,64]{3,2,1,0:T(8,128)}, u32[]{:S(2)}, u32[]{:S(2)}) collective-permute-start(f32[2,7,64,64]{3,2,1,0:T(8,128)} %multiply_add_fusion.2), channel_id=1, source_target_pairs={{0,8},{8,16},{16,24},{24,32},{32,40},{40,48},{48,56},{56,64},{64,7... | collective-permute-start | bytes 688136 | tf_op jit(solution)/shard_map/while/body/eval_jaxpr/ppermute | solution.py:12
  372.5 12.9 %collective-permute-start = (f32[2,7,64,64]{3,2,1,0:T(8,128)}, f32[2,7,64,64]{3,2,1,0:T(8,128)}, u32[]{:S(2)}, u32[]{:S(2)}) collective-permute-start(f32[2,7,64,64]{3,2,1,0:T(8,128)} %multiply_add_fusion.2), channel_id=1, source_target_pairs={{0,8},{8,16},{16,24},{24,32},{32,40},{40,48},{48,56},{56,64},{64,7... | collective-permute-start | bytes 688136 | tf_op jit(solution)/shard_map/while/body/eval_jaxpr/ppermute | solution.py:12
  387.4 12.8 %collective-permute-start = (f32[2,7,64,64]{3,2,1,0:T(8,128)}, f32[2,7,64,64]{3,2,1,0:T(8,128)}, u32[]{:S(2)}, u32[]{:S(2)}) collective-permute-start(f32[2,7,64,64]{3,2,1,0:T(8,128)} %multiply_add_fusion.2), channel_id=1, source_target_pairs={{0,8},{8,16},{16,24},{24,32},{32,40},{40,48},{48,56},{56,64},{64,7... | collective-permute-start | bytes 688136 | tf_op jit(solution)/shard_map/while/body/eval_jaxpr/ppermute | solution.py:12
  402.3 12.8 %collective-permute-start = (f32[2,7,64,64]{3,2,1,0:T(8,128)}, f32[2,7,64,64]{3,2,1,0:T(8,128)}, u32[]{:S(2)}, u32[]{:S(2)}) collective-permute-start(f32[2,7,64,64]{3,2,1,0:T(8,128)} %multiply_add_fusion.2), channel_id=1, source_target_pairs={{0,8},{8,16},{16,24},{24,32},{32,40},{40,48},{48,56},{56,64},{64,7... | collective-permute-start | bytes 688136 | tf_op jit(solution)/shard_map/while/body/eval_jaxpr/ppermute | solution.py:12
  417.1 12.8 %collective-permute-start = (f32[2,7,64,64]{3,2,1,0:T(8,128)}, f32[2,7,64,64]{3,2,1,0:T(8,128)}, u32[]{:S(2)}, u32[]{:S(2)}) collective-permute-start(f32[2,7,64,64]{3,2,1,0:T(8,128)} %multiply_add_fusion.2), channel_id=1, source_target_pairs={{0,8},{8,16},{16,24},{24,32},{32,40},{40,48},{48,56},{56,64},{64,7... | collective-permute-start | bytes 688136 | tf_op jit(solution)/shard_map/while/body/eval_jaxpr/ppermute | solution.py:12
  431.9 12.8 %collective-permute-start = (f32[2,7,64,64]{3,2,1,0:T(8,128)}, f32[2,7,64,64]{3,2,1,0:T(8,128)}, u32[]{:S(2)}, u32[]{:S(2)}) collective-permute-start(f32[2,7,64,64]{3,2,1,0:T(8,128)} %multiply_add_fusion.2), channel_id=1, source_target_pairs={{0,8},{8,16},{16,24},{24,32},{32,40},{40,48},{48,56},{56,64},{64,7... | collective-permute-start | bytes 688136 | tf_op jit(solution)/shard_map/while/body/eval_jaxpr/ppermute | solution.py:12
  446.8 13.4 %collective-permute-start = (f32[2,7,64,64]{3,2,1,0:T(8,128)}, f32[2,7,64,64]{3,2,1,0:T(8,128)}, u32[]{:S(2)}, u32[]{:S(2)}) collective-permute-start(f32[2,7,64,64]{3,2,1,0:T(8,128)} %multiply_add_fusion.2), channel_id=1, source_target_pairs={{0,8},{8,16},{16,24},{24,32},{32,40},{40,48},{48,56},{56,64},{64,7... | collective-permute-start | bytes 688136 | tf_op jit(solution)/shard_map/while/body/eval_jaxpr/ppermute | solution.py:12
  462.2 14.7 %collective-permute-start = (f32[2,7,64,64]{3,2,1,0:T(8,128)}, f32[2,7,64,64]{3,2,1,0:T(8,128)}, u32[]{:S(2)}, u32[]{:S(2)}) collective-permute-start(f32[2,7,64,64]{3,2,1,0:T(8,128)} %multiply_add_fusion.2), channel_id=1, source_target_pairs={{0,8},{8,16},{16,24},{24,32},{32,40},{40,48},{48,56},{56,64},{64,7... | collective-permute-start | bytes 688136 | tf_op jit(solution)/shard_map/while/body/eval_jaxpr/ppermute | solution.py:12
  479.0 16.4 %collective-permute-start = (f32[2,7,64,64]{3,2,1,0:T(8,128)}, f32[2,7,64,64]{3,2,1,0:T(8,128)}, u32[]{:S(2)}, u32[]{:S(2)}) collective-permute-start(f32[2,7,64,64]{3,2,1,0:T(8,128)} %multiply_add_fusion.2), channel_id=1, source_target_pairs={{0,8},{8,16},{16,24},{24,32},{32,40},{40,48},{48,56},{56,64},{64,7... | collective-permute-start | bytes 688136 | tf_op jit(solution)/shard_map/while/body/eval_jaxpr/ppermute | solution.py:12
  497.4 17.5 %collective-permute-start = (f32[2,7,64,64]{3,2,1,0:T(8,128)}, f32[2,7,64,64]{3,2,1,0:T(8,128)}, u32[]{:S(2)}, u32[]{:S(2)}) collective-permute-start(f32[2,7,64,64]{3,2,1,0:T(8,128)} %multiply_add_fusion.2), channel_id=1, source_target_pairs={{0,8},{8,16},{16,24},{24,32},{32,40},{40,48},{48,56},{56,64},{64,7... | collective-permute-start | bytes 688136 | tf_op jit(solution)/shard_map/while/body/eval_jaxpr/ppermute | solution.py:12
  517.0 18.5 %collective-permute-start = (f32[2,7,64,64]{3,2,1,0:T(8,128)}, f32[2,7,64,64]{3,2,1,0:T(8,128)}, u32[]{:S(2)}, u32[]{:S(2)}) collective-permute-start(f32[2,7,64,64]{3,2,1,0:T(8,128)} %multiply_add_fusion.2), channel_id=1, source_target_pairs={{0,8},{8,16},{16,24},{24,32},{32,40},{40,48},{48,56},{56,64},{64,7... | collective-permute-start | bytes 688136 | tf_op jit(solution)/shard_map/while/body/eval_jaxpr/ppermute | solution.py:12
  537.5 16.7 %collective-permute-start = (f32[2,7,64,64]{3,2,1,0:T(8,128)}, f32[2,7,64,64]{3,2,1,0:T(8,128)}, u32[]{:S(2)}, u32[]{:S(2)}) collective-permute-start(f32[2,7,64,64]{3,2,1,0:T(8,128)} %multiply_add_fusion.2), channel_id=1, source_target_pairs={{0,8},{8,16},{16,24},{24,32},{32,40},{40,48},{48,56},{56,64},{64,7... | collective-permute-start | bytes 688136 | tf_op jit(solution)/shard_map/while/body/eval_jaxpr/ppermute | solution.py:12
  556.3 15.0 %collective-permute-start = (f32[2,7,64,64]{3,2,1,0:T(8,128)}, f32[2,7,64,64]{3,2,1,0:T(8,128)}, u32[]{:S(2)}, u32[]{:S(2)}) collective-permute-start(f32[2,7,64,64]{3,2,1,0:T(8,128)} %multiply_add_fusion.2), channel_id=1, source_target_pairs={{0,8},{8,16},{16,24},{24,32},{32,40},{40,48},{48,56},{56,64},{64,7... | collective-permute-start | bytes 688136 | tf_op jit(solution)/shard_map/while/body/eval_jaxpr/ppermute | solution.py:12
  573.4 13.7 %collective-permute-start = (f32[2,7,64,64]{3,2,1,0:T(8,128)}, f32[2,7,64,64]{3,2,1,0:T(8,128)}, u32[]{:S(2)}, u32[]{:S(2)}) collective-permute-start(f32[2,7,64,64]{3,2,1,0:T(8,128)} %multiply_add_fusion.2), channel_id=1, source_target_pairs={{0,8},{8,16},{16,24},{24,32},{32,40},{40,48},{48,56},{56,64},{64,7... | collective-permute-start | bytes 688136 | tf_op jit(solution)/shard_map/while/body/eval_jaxpr/ppermute | solution.py:12
  589.1 12.8 %collective-permute-start = (f32[2,7,64,64]{3,2,1,0:T(8,128)}, f32[2,7,64,64]{3,2,1,0:T(8,128)}, u32[]{:S(2)}, u32[]{:S(2)}) collective-permute-start(f32[2,7,64,64]{3,2,1,0:T(8,128)} %multiply_add_fusion.2), channel_id=1, source_target_pairs={{0,8},{8,16},{16,24},{24,32},{32,40},{40,48},{48,56},{56,64},{64,7... | collective-permute-start | bytes 688136 | tf_op jit(solution)/shard_map/while/body/eval_jaxpr/ppermute | solution.py:12
  603.9 12.8 %collective-permute-start = (f32[2,7,64,64]{3,2,1,0:T(8,128)}, f32[2,7,64,64]{3,2,1,0:T(8,128)}, u32[]{:S(2)}, u32[]{:S(2)}) collective-permute-start(f32[2,7,64,64]{3,2,1,0:T(8,128)} %multiply_add_fusion.2), channel_id=1, source_target_pairs={{0,8},{8,16},{16,24},{24,32},{32,40},{40,48},{48,56},{56,64},{64,7... | collective-permute-start | bytes 688136 | tf_op jit(solution)/shard_map/while/body/eval_jaxpr/ppermute | solution.py:12
  616.7 2.4 copy-start.6
  619.4 0.8 copy-start.3
  622.3 3.0 copy-start.1
  625.3 1.5 copy-start.8
  635.5 85.0 %copy-start.9 = (f32[3584]{0:T(1024)S(1)}, f32[3584]{0:T(1024)}, u32[]{:S(2)}) copy-start(f32[3584]{0:T(1024)} %param.38) | copy-start | bytes 43012
  635.5 87.7 %copy-start.18 = (u32[256]{0:T(256)S(1)}, u32[256]{0:T(256)}, u32[]{:S(2)}) copy-start(u32[256]{0:T(256)} %constant.72) | copy-start | bytes 3076
  635.5 88.3 %copy-start.12 = (s32[256]{0:T(256)S(1)}, s32[256]{0:T(256)}, u32[]{:S(2)}) copy-start(s32[256]{0:T(256)} %param.21) | copy-start | bytes 3076
  635.5 118.4 %all-gather.6.cloned.1.call-start = ((), (), s32[]{:S(2)}) async-start(), calls=%async_computation.3 | async-start | bytes 4128768 | tf_op jit(solution)/shard_map/all_gather | solution.py:132
  722.6 163.8 %all-gather.8.cloned.1.call-start = ((), (), s32[]{:S(2)}) async-start(), calls=%async_computation.4 | async-start | bytes 15138816 | tf_op jit(solution)/shard_map/all_gather | solution.py:137
  900.0 29.5 %copy-start.13 = (s32[256]{0:T(256)S(1)}, s32[256]{0:T(256)}, u32[]{:S(2)}) copy-start(s32[256]{0:T(256)} %param.22) | copy-start | bytes 3076
  900.0 29.5 %copy-start.16 = (s32[48]{0:T(128)S(1)}, s32[48]{0:T(128)}, u32[]{:S(2)}) copy-start(s32[48]{0:T(128)} %param.23) | copy-start | bytes 580
  900.0 29.6 %copy-start.17 = (s32[48]{0:T(128)S(1)}, s32[48]{0:T(128)}, u32[]{:S(2)}) copy-start(s32[48]{0:T(128)} %param.24) | copy-start | bytes 580
  929.5 140.7 %copy-start.14 = (f32[256]{0:T(256)}, f32[256]{0:T(256)S(1)}, u32[]{:S(2)}) copy-start(f32[256]{0:T(256)S(1)} %convert_multiply_fusion.4) | copy-start | bytes 3076
Sparse Core Ops, SparseCore 0:
  10.6 94.5 all-gather.3
  635.6 83.3 reduce-scatter.1
  722.7 31.2 all-gather.5
  756.4 129.9 all-gather.7
where the time goes:
time: 1080 us
  waiting for transfers between devices  533 us (49%)
  starting transfers between devices  215 us (20%)
  blocking collectives  166 us (15%)
  other arithmetic  88.2 us (8%)
  matrix products  41 us (4%)
  local copies, waits for them, and re-layouts  18.2 us (2%)
  between operations  14.6 us (1%)
    ppermute x31, waiting for transfers between devices, shifted(): return lax.ppermute(x, axis, pairs)  220 us
    ppermute x31, starting transfers between devices, shifted(): return lax.ppermute(x, axis, pairs)  215 us
    unnamed x1, blocking collectives  139 us
    all_gather x1, waiting for transfers between devices, shards(): lax.all_gather(vocab_head_weight, 'seq', axis=0, tiled=True)  132 us
    reduce_scatter x1, waiting for transfers between devices, shards(): lax.psum_scatter(jnp.stack([base_output[:, 0] + adapter_output, base_outp...  81.4 us
    all_gather x1, waiting for transfers between devices, shards(): piece = lax.all_gather(prompt_held_states, 'seq', axis=1, tiled=True)  69.4 us
    add x31, other arithmetic, relay_step(): outgoing = carry_through[:, :, None, None] * incoming + local_end  63.3 us
    all_gather x1, waiting for transfers between devices, shards(): normed = lax.all_gather(normed_own, 'mp', axis=0, tiled=True)  28.5 us
  transfers between devices with their start and end apart: 35, of which 35 were waited for; matrix products, arithmetic and copies ran while one was open for 3% of the time, Pallas kernels for 0%

commit v1 on v0

--- a/solution.py
+++ b/solution.py
@@ -129,7 +129,16 @@
     ).astype(jnp.float32)
     own_rows = lax.dynamic_slice_in_dim(residual, lax.axis_index("mp") * share_rows, share_rows, 0)
     normed_own = root_norm(own_rows.astype(jnp.float32) + mixed, final_norm_scale)
-    normed = lax.all_gather(normed_own, "mp", axis=0, tiled=True)
+    ways = lax.axis_size("mp")
+    up = [(d, (d + 1) % ways) for d in range(ways)]
+    down = [(d, (d - 1) % ways) for d in range(ways)]
+    earlier, later = ([normed_own], [normed_own])
+    for _ in range(ways // 2):
+        earlier.append(lax.ppermute(earlier[-1], "mp", up))
+    for _ in range((ways - 1) // 2):
+        later.append(lax.ppermute(later[-1], "mp", down))
+    line = jnp.concatenate([*earlier[::-1], *later[1:]], axis=0)
+    normed = jnp.roll(line, (lax.axis_index("mp") - ways // 2) * normed_own.shape[0], axis=0)
     vocab_local = vocab_head_weight.shape[1]
     logits = jnp.einsum(
         "tmk,kv->mtv",

time: 1080 us -> 1040 us (0.963)
  waiting for transfers between devices: 533 us -> 477 us
  local copies, waits for them, and re-layouts: 18.2 us -> 29 us
    all_gather x1, waiting for transfers between devices: 132 us -> 79.6 us  [shards(): lax.all_gather(vocab_head_weight, 'seq', axis=0, tiled=True)]
    all_gather x1 -> x0, waiting for transfers between devices: 28.5 us -> none  [shards(): normed = lax.all_gather(normed_own, 'mp', axis=0, tiled=True)]
    ppermute x0 -> x7, waiting for transfers between devices: none -> 25.3 us  [the longest x4 25.3 us: shards(): earlier.append(lax.ppermute(earlier[-1], 'mp', up))]
    unnamed x41 -> x56, local copies, waits for them, and re-layouts: 6.97 us -> 19.1 us
  transfers between devices with their start and end apart: 35 -> 41, of which waited for: 35 -> 38; matrix products, arithmetic and copies ran while one was open for 3% -> 4% of each run, Pallas kernels for 0% -> 0%
where the time goes in v1:
time: 1040 us
  waiting for transfers between devices  477 us (46%)
  starting transfers between devices  224 us (22%)
  blocking collectives  166 us (16%)
  other arithmetic  87.7 us (8%)
  matrix products  41.2 us (4%)
  local copies, waits for them, and re-layouts  29 us (3%)
  between operations  14.6 us (1%)
    ppermute x31, waiting for transfers between devices, shifted(): return lax.ppermute(x, axis, pairs)  220 us
    ppermute x31, starting transfers between devices, shifted(): return lax.ppermute(x, axis, pairs)  215 us
    unnamed x1, blocking collectives  139 us
    reduce_scatter x1, waiting for transfers between devices, shards(): lax.psum_scatter(jnp.stack([base_output[:, 0] + adapter_output, base_outp...  81.5 us
    all_gather x1, waiting for transfers between devices, shards(): lax.all_gather(vocab_head_weight, 'seq', axis=0, tiled=True)  79.6 us
    all_gather x1, waiting for transfers between devices, shards(): piece = lax.all_gather(prompt_held_states, 'seq', axis=1, tiled=True)  69.4 us
    add x31, other arithmetic, relay_step(): outgoing = carry_through[:, :, None, None] * incoming + local_end  63.3 us
    ppermute x4, waiting for transfers between devices, shards(): earlier.append(lax.ppermute(earlier[-1], 'mp', up))  25.3 us
  transfers between devices with their start and end apart: 41, of which 38 were waited for; matrix products, arithmetic and copies ran while one was open for 4% of the time, Pallas kernels for 0%

profile of v1, /device:TPU:0, one launch (start us, length us, event | category | flops | bytes accessed | tf_op | source)
XLA Modules:
  0.0 1040.1 jit_solution(14838279720373486931)
XLA Ops:
  35.8 69.4 %all-gather.3.cloned.1.call-done = bf16[2,32,7,64,64]{4,3,1,2,0:T(8,128)(2,1)} async-done(((bf16[2,1,7,64,64]{4,3,1,2,0:T(8,128)(2,1)}), bf16[2,32,7,64,64]{4,3,1,2,0:T(8,128)(2,1)}) %all-gather.3.cloned.1.call-update) | async-done | bytes 3670032 | tf_op jit(solution)/shard_map/all_gather | solution.py:81
  105.2 7.4 fusion.2
  117.8 498.9 %while.10 = (s32[]{:T(128)}, f32[2,7,64,64]{3,2,1,0:T(8,128)}, f32[2,7]{1,0:T(2,128)S(1)}, f32[2,7,64,64]{3,2,1,0:T(8,128)}, s32[]{:T(128)}) while((s32[]{:T(128)}, f32[2,7,64,64]{3,2,1,0:T(8,128)}, f32[2,7]{1,0:T(2,128)S(1)}, f32[2,7,64,64]{3,2,1,0:T(8,128)}, s32[]{:T(128)}) %tuple.33), condition=%wide.region_7.8_spmd, body=%wide.region_6.7_spmd.sunk | while | flops 114690 | bytes 1605789 | solution.py:102
  122.8 8.9 collective-permute-done
  138.9 7.9 collective-permute-done
  154.1 7.0 collective-permute-done
  168.3 6.1 collective-permute-done
  181.6 5.5 collective-permute-done
  194.4 5.5 collective-permute-done
  201.9 5.9 collective-permute-start
  207.8 5.5 collective-permute-done
  215.3 7.3 collective-permute-start
  222.6 5.5 collective-permute-done
  230.1 7.5 collective-permute-start
  237.6 6.4 collective-permute-done
  246.1 7.9 collective-permute-start
  254.0 7.5 collective-permute-done
  263.5 8.2 collective-permute-start
  271.7 8.6 collective-permute-done
  282.3 8.2 collective-permute-start
  290.5 9.8 collective-permute-done
  302.4 8.2 collective-permute-start
  310.6 9.9 collective-permute-done
  322.5 7.6 collective-permute-start
  330.1 8.7 collective-permute-done
  340.8 6.4 collective-permute-start
  347.2 7.4 collective-permute-done
  356.7 7.3 collective-permute-start
  364.0 6.5 collective-permute-done
  372.5 7.3 collective-permute-start
  379.8 5.6 collective-permute-done
  387.4 7.3 collective-permute-start
  402.3 7.3 collective-permute-start
  417.1 7.3 collective-permute-start
  431.9 7.3 collective-permute-start
  439.2 5.5 collective-permute-done
  446.8 7.3 collective-permute-start
  454.1 6.1 collective-permute-done
  462.2 7.6 collective-permute-start
  469.8 7.1 collective-permute-done
  479.0 8.2 collective-permute-start
  487.1 8.2 collective-permute-done
  497.4 8.2 collective-permute-start
  505.6 9.3 collective-permute-done
  517.0 8.2 collective-permute-start
  525.2 10.3 collective-permute-done
  537.5 7.6 collective-permute-start
  545.1 9.1 collective-permute-done
  556.3 7.1 collective-permute-start
  563.4 8.0 collective-permute-done
  573.4 6.8 collective-permute-start
  580.2 6.9 collective-permute-done
  589.1 7.3 collective-permute-start
  596.4 5.5 collective-permute-done
  603.9 7.3 collective-permute-start
  611.2 5.5 collective-permute-done
  636.8 81.5 %reduce-scatter.2.cloned.1.call-done = bf16[32,2,3584]{2,0,1:T(8,128)(2,1)} async-done(((bf16[256,2,3584]{2,0,1:T(8,128)(2,1)}), bf16[32,2,3584]{2,0,1:T(8,128)(2,1)}) %reduce-scatter.2.cloned.1.call-update) | async-done | bytes 458768 | tf_op jit(solution)/shard_map/reduce_scatter | solution.py:122
  720.7 9.1 collective-permute-done.1
  732.8 6.2 collective-permute-done.2
  770.1 79.6 %all-gather.5.cloned.1.call-done = bf16[3584,2000]{1,0:T(8,128)(2,1)} async-done(((bf16[112,2000]{1,0:T(8,128)(2,1)}), bf16[3584,2000]{1,0:T(8,128)(2,1)}) %all-gather.5.cloned.1.call-update) | async-done | bytes 14336016 | tf_op jit(solution)/shard_map/all_gather | solution.py:146
  849.7 13.8 %fusion.6 = (f32[2,256]{1,0:T(2,128)S(1)}, f32[2,256]{1,0:T(2,128)S(1)}, f32[256,2,2000]{0,2,1:T(8,128)}) fusion(pred[256,2000]{0,1:T(8,128)(4,1)} %broadcast_compare_fusion, bf16[3584,2000]{1,0:T(8,128)(2,1)} %all-gather.5.cloned.1.call-done, bf16[512,2,3584]{2,0,1:T(8,128)(2,1)} %constant_dynamic-update-slice_fusion, s32[]{:T(128)S(6)} %select_n.63), kind=kOutput, calls=%fused_computation.14 | convolution fusion | flops 7343102976 | bytes 22962180 | tf_op jit(solution)/shard_map/tmk,kv->mtv/dot_general | solution.py:143
  863.6 14.2 %pmax.7 = f32[2,256]{1,0:T(2,128)S(1)} all-reduce(f32[2,256]{1,0:T(2,128)S(1)} %get-tuple-element.26), channel_id=1, replica_groups=mesh['seq'=32,'mp'=8] {'mp'}, use_global_device_ids=true, to_apply=%region_13.14 | all-reduce | flops 512 | bytes 4096 | tf_op jit(solution)/shard_map/pmax | solution.py:156
  880.4 12.4 %all-reduce.1 = (f32[2,256]{1,0:T(2,128)S(1)}, f32[2,256]{1,0:T(2,128)S(1)}) all-reduce(f32[2,256]{1,0:T(2,128)S(1)} %fusion.8, f32[2,256]{1,0:T(2,128)S(1)} %get-tuple-element.25), channel_id=1, replica_groups=mesh['seq'=32,'mp'=8] {'mp'}, use_global_device_ids=true, to_apply=%region_15.16 | all-reduce | flops 1024 | bytes 8192 | tf_op jit(solution)/shard_map/psum | solution.py:158
  893.1 139.3 %all-reduce = f32[32,48]{1,0:T(8,128)S(1)} all-reduce(f32[32,48]{1,0:T(8,128)S(1)} %fusion.55), channel_id=3, replica_groups=mesh['seq'=32,'mp'=8] {'seq'}, use_global_device_ids=true, to_apply=%region_16.17.clone | all-reduce | flops 1536 | bytes 12288
  (184 shorter events, 202.5 us)
Async XLA Ops:
  7.2 614.0 %copy-start = (bf16[448,3584]{1,0:T(8,128)(2,1)S(1)}, bf16[448,3584]{1,0:T(8,128)(2,1)}, u32[]{:S(2)}) copy-start(bf16[448,3584]{1,0:T(8,128)(2,1)} %param.34) | copy-start | bytes 9633796
  7.2 98.0 %all-gather.3.cloned.1.call-start = ((), (), s32[]{:S(2)}) async-start(), calls=%async_computation.1 | async-start | bytes 7569408 | tf_op jit(solution)/shard_map/all_gather | solution.py:81
  7.9 710.4 %reduce-scatter.2.cloned.1.call-start = ((), (), s32[]{:S(2)}) async-start(), calls=%async_computation.2 | async-start | bytes 4128768 | tf_op jit(solution)/shard_map/reduce_scatter | solution.py:122
  19.7 4.8 copy-start.11
  30.4 82.1 %copy-start.7 = (bf16[2,256,64]{1,2,0:T(8,128)(2,1)S(1)}, bf16[2,256,64]{1,2,0:T(8,128)(2,1)}, u32[]{:S(2)}) copy-start(bf16[2,256,64]{1,2,0:T(8,128)(2,1)} %param.28) | copy-start | bytes 196612
  30.5 83.5 %copy-start.10 = (f32[2,256,7]{1,2,0:T(8,128)S(1)}, f32[2,256,7]{1,2,0:T(8,128)}, u32[]{:S(2)}) copy-start(f32[2,256,7]{1,2,0:T(8,128)} %copy.130) | copy-start | bytes 43012
  105.2 7.4 copy-start.5
  105.2 8.8 copy-start.3
  117.0 499.8 %copy-start.6 = (bf16[2,256,64]{1,2,0:T(8,128)(2,1)S(1)}, bf16[2,256,64]{1,2,0:T(8,128)(2,1)}, u32[]{:S(2)}) copy-start(bf16[2,256,64]{1,2,0:T(8,128)(2,1)} %param.29) | copy-start | bytes 196612
  117.0 499.8 %copy-start.15 = (f32[2,7]{1,0:T(2,128)S(1)}, f32[2,7]{1,0:T(2,128)}, u32[]{:S(2)}) copy-start(f32[2,7]{1,0:T(2,128)} %param.32) | copy-start | bytes 172
  119.9 11.8 %collective-permute-start = (f32[2,7,64,64]{3,2,1,0:T(8,128)}, f32[2,7,64,64]{3,2,1,0:T(8,128)}, u32[]{:S(2)}, u32[]{:S(2)}) collective-permute-start(f32[2,7,64,64]{3,2,1,0:T(8,128)} %multiply_add_fusion.2), channel_id=1, source_target_pairs={{0,8},{8,16},{16,24},{24,32},{32,40},{40,48},{48,56},{56,64},{64,7... | collective-permute-start | bytes 688136 | tf_op jit(solution)/shard_map/while/body/eval_jaxpr/ppermute | solution.py:12
  133.7 13.1 %collective-permute-start = (f32[2,7,64,64]{3,2,1,0:T(8,128)}, f32[2,7,64,64]{3,2,1,0:T(8,128)}, u32[]{:S(2)}, u32[]{:S(2)}) collective-permute-start(f32[2,7,64,64]{3,2,1,0:T(8,128)} %multiply_add_fusion.2), channel_id=1, source_target_pairs={{0,8},{8,16},{16,24},{24,32},{32,40},{40,48},{48,56},{56,64},{64,7... | collective-permute-start | bytes 688136 | tf_op jit(solution)/shard_map/while/body/eval_jaxpr/ppermute | solution.py:12
  148.9 12.2 %collective-permute-start = (f32[2,7,64,64]{3,2,1,0:T(8,128)}, f32[2,7,64,64]{3,2,1,0:T(8,128)}, u32[]{:S(2)}, u32[]{:S(2)}) collective-permute-start(f32[2,7,64,64]{3,2,1,0:T(8,128)} %multiply_add_fusion.2), channel_id=1, source_target_pairs={{0,8},{8,16},{16,24},{24,32},{32,40},{40,48},{48,56},{56,64},{64,7... | collective-permute-start | bytes 688136 | tf_op jit(solution)/shard_map/while/body/eval_jaxpr/ppermute | solution.py:12
  163.1 11.3 %collective-permute-start = (f32[2,7,64,64]{3,2,1,0:T(8,128)}, f32[2,7,64,64]{3,2,1,0:T(8,128)}, u32[]{:S(2)}, u32[]{:S(2)}) collective-permute-start(f32[2,7,64,64]{3,2,1,0:T(8,128)} %multiply_add_fusion.2), channel_id=1, source_target_pairs={{0,8},{8,16},{16,24},{24,32},{32,40},{40,48},{48,56},{56,64},{64,7... | collective-permute-start | bytes 688136 | tf_op jit(solution)/shard_map/while/body/eval_jaxpr/ppermute | solution.py:12
  176.4 10.7 %collective-permute-start = (f32[2,7,64,64]{3,2,1,0:T(8,128)}, f32[2,7,64,64]{3,2,1,0:T(8,128)}, u32[]{:S(2)}, u32[]{:S(2)}) collective-permute-start(f32[2,7,64,64]{3,2,1,0:T(8,128)} %multiply_add_fusion.2), channel_id=1, source_target_pairs={{0,8},{8,16},{16,24},{24,32},{32,40},{40,48},{48,56},{56,64},{64,7... | collective-permute-start | bytes 688136 | tf_op jit(solution)/shard_map/while/body/eval_jaxpr/ppermute | solution.py:12
  189.2 10.7 %collective-permute-start = (f32[2,7,64,64]{3,2,1,0:T(8,128)}, f32[2,7,64,64]{3,2,1,0:T(8,128)}, u32[]{:S(2)}, u32[]{:S(2)}) collective-permute-start(f32[2,7,64,64]{3,2,1,0:T(8,128)} %multiply_add_fusion.2), channel_id=1, source_target_pairs={{0,8},{8,16},{16,24},{24,32},{32,40},{40,48},{48,56},{56,64},{64,7... | collective-permute-start | bytes 688136 | tf_op jit(solution)/shard_map/while/body/eval_jaxpr/ppermute | solution.py:12
  201.9 11.4 %collective-permute-start = (f32[2,7,64,64]{3,2,1,0:T(8,128)}, f32[2,7,64,64]{3,2,1,0:T(8,128)}, u32[]{:S(2)}, u32[]{:S(2)}) collective-permute-start(f32[2,7,64,64]{3,2,1,0:T(8,128)} %multiply_add_fusion.2), channel_id=1, source_target_pairs={{0,8},{8,16},{16,24},{24,32},{32,40},{40,48},{48,56},{56,64},{64,7... | collective-permute-start | bytes 688136 | tf_op jit(solution)/shard_map/while/body/eval_jaxpr/ppermute | solution.py:12
  215.3 12.8 %collective-permute-start = (f32[2,7,64,64]{3,2,1,0:T(8,128)}, f32[2,7,64,64]{3,2,1,0:T(8,128)}, u32[]{:S(2)}, u32[]{:S(2)}) collective-permute-start(f32[2,7,64,64]{3,2,1,0:T(8,128)} %multiply_add_fusion.2), channel_id=1, source_target_pairs={{0,8},{8,16},{16,24},{24,32},{32,40},{40,48},{48,56},{56,64},{64,7... | collective-permute-start | bytes 688136 | tf_op jit(solution)/shard_map/while/body/eval_jaxpr/ppermute | solution.py:12
  230.1 13.9 %collective-permute-start = (f32[2,7,64,64]{3,2,1,0:T(8,128)}, f32[2,7,64,64]{3,2,1,0:T(8,128)}, u32[]{:S(2)}, u32[]{:S(2)}) collective-permute-start(f32[2,7,64,64]{3,2,1,0:T(8,128)} %multiply_add_fusion.2), channel_id=1, source_target_pairs={{0,8},{8,16},{16,24},{24,32},{32,40},{40,48},{48,56},{56,64},{64,7... | collective-permute-start | bytes 688136 | tf_op jit(solution)/shard_map/while/body/eval_jaxpr/ppermute | solution.py:12
  246.1 15.4 %collective-permute-start = (f32[2,7,64,64]{3,2,1,0:T(8,128)}, f32[2,7,64,64]{3,2,1,0:T(8,128)}, u32[]{:S(2)}, u32[]{:S(2)}) collective-permute-start(f32[2,7,64,64]{3,2,1,0:T(8,128)} %multiply_add_fusion.2), channel_id=1, source_target_pairs={{0,8},{8,16},{16,24},{24,32},{32,40},{40,48},{48,56},{56,64},{64,7... | collective-permute-start | bytes 688136 | tf_op jit(solution)/shard_map/while/body/eval_jaxpr/ppermute | solution.py:12
  263.5 16.8 %collective-permute-start = (f32[2,7,64,64]{3,2,1,0:T(8,128)}, f32[2,7,64,64]{3,2,1,0:T(8,128)}, u32[]{:S(2)}, u32[]{:S(2)}) collective-permute-start(f32[2,7,64,64]{3,2,1,0:T(8,128)} %multiply_add_fusion.2), channel_id=1, source_target_pairs={{0,8},{8,16},{16,24},{24,32},{32,40},{40,48},{48,56},{56,64},{64,7... | collective-permute-start | bytes 688136 | tf_op jit(solution)/shard_map/while/body/eval_jaxpr/ppermute | solution.py:12
  282.3 18.0 %collective-permute-start = (f32[2,7,64,64]{3,2,1,0:T(8,128)}, f32[2,7,64,64]{3,2,1,0:T(8,128)}, u32[]{:S(2)}, u32[]{:S(2)}) collective-permute-start(f32[2,7,64,64]{3,2,1,0:T(8,128)} %multiply_add_fusion.2), channel_id=1, source_target_pairs={{0,8},{8,16},{16,24},{24,32},{32,40},{40,48},{48,56},{56,64},{64,7... | collective-permute-start | bytes 688136 | tf_op jit(solution)/shard_map/while/body/eval_jaxpr/ppermute | solution.py:12
  302.4 18.1 %collective-permute-start = (f32[2,7,64,64]{3,2,1,0:T(8,128)}, f32[2,7,64,64]{3,2,1,0:T(8,128)}, u32[]{:S(2)}, u32[]{:S(2)}) collective-permute-start(f32[2,7,64,64]{3,2,1,0:T(8,128)} %multiply_add_fusion.2), channel_id=1, source_target_pairs={{0,8},{8,16},{16,24},{24,32},{32,40},{40,48},{48,56},{56,64},{64,7... | collective-permute-start | bytes 688136 | tf_op jit(solution)/shard_map/while/body/eval_jaxpr/ppermute | solution.py:12
  322.5 16.2 %collective-permute-start = (f32[2,7,64,64]{3,2,1,0:T(8,128)}, f32[2,7,64,64]{3,2,1,0:T(8,128)}, u32[]{:S(2)}, u32[]{:S(2)}) collective-permute-start(f32[2,7,64,64]{3,2,1,0:T(8,128)} %multiply_add_fusion.2), channel_id=1, source_target_pairs={{0,8},{8,16},{16,24},{24,32},{32,40},{40,48},{48,56},{56,64},{64,7... | collective-permute-start | bytes 688136 | tf_op jit(solution)/shard_map/while/body/eval_jaxpr/ppermute | solution.py:12
  340.8 13.8 %collective-permute-start = (f32[2,7,64,64]{3,2,1,0:T(8,128)}, f32[2,7,64,64]{3,2,1,0:T(8,128)}, u32[]{:S(2)}, u32[]{:S(2)}) collective-permute-start(f32[2,7,64,64]{3,2,1,0:T(8,128)} %multiply_add_fusion.2), channel_id=1, source_target_pairs={{0,8},{8,16},{16,24},{24,32},{32,40},{40,48},{48,56},{56,64},{64,7... | collective-permute-start | bytes 688136 | tf_op jit(solution)/shard_map/while/body/eval_jaxpr/ppermute | solution.py:12
  356.7 13.8 %collective-permute-start = (f32[2,7,64,64]{3,2,1,0:T(8,128)}, f32[2,7,64,64]{3,2,1,0:T(8,128)}, u32[]{:S(2)}, u32[]{:S(2)}) collective-permute-start(f32[2,7,64,64]{3,2,1,0:T(8,128)} %multiply_add_fusion.2), channel_id=1, source_target_pairs={{0,8},{8,16},{16,24},{24,32},{32,40},{40,48},{48,56},{56,64},{64,7... | collective-permute-start | bytes 688136 | tf_op jit(solution)/shard_map/while/body/eval_jaxpr/ppermute | solution.py:12
  372.5 12.9 %collective-permute-start = (f32[2,7,64,64]{3,2,1,0:T(8,128)}, f32[2,7,64,64]{3,2,1,0:T(8,128)}, u32[]{:S(2)}, u32[]{:S(2)}) collective-permute-start(f32[2,7,64,64]{3,2,1,0:T(8,128)} %multiply_add_fusion.2), channel_id=1, source_target_pairs={{0,8},{8,16},{16,24},{24,32},{32,40},{40,48},{48,56},{56,64},{64,7... | collective-permute-start | bytes 688136 | tf_op jit(solution)/shard_map/while/body/eval_jaxpr/ppermute | solution.py:12
  387.4 12.8 %collective-permute-start = (f32[2,7,64,64]{3,2,1,0:T(8,128)}, f32[2,7,64,64]{3,2,1,0:T(8,128)}, u32[]{:S(2)}, u32[]{:S(2)}) collective-permute-start(f32[2,7,64,64]{3,2,1,0:T(8,128)} %multiply_add_fusion.2), channel_id=1, source_target_pairs={{0,8},{8,16},{16,24},{24,32},{32,40},{40,48},{48,56},{56,64},{64,7... | collective-permute-start | bytes 688136 | tf_op jit(solution)/shard_map/while/body/eval_jaxpr/ppermute | solution.py:12
  402.3 12.8 %collective-permute-start = (f32[2,7,64,64]{3,2,1,0:T(8,128)}, f32[2,7,64,64]{3,2,1,0:T(8,128)}, u32[]{:S(2)}, u32[]{:S(2)}) collective-permute-start(f32[2,7,64,64]{3,2,1,0:T(8,128)} %multiply_add_fusion.2), channel_id=1, source_target_pairs={{0,8},{8,16},{16,24},{24,32},{32,40},{40,48},{48,56},{56,64},{64,7... | collective-permute-start | bytes 688136 | tf_op jit(solution)/shard_map/while/body/eval_jaxpr/ppermute | solution.py:12
  417.1 12.8 %collective-permute-start = (f32[2,7,64,64]{3,2,1,0:T(8,128)}, f32[2,7,64,64]{3,2,1,0:T(8,128)}, u32[]{:S(2)}, u32[]{:S(2)}) collective-permute-start(f32[2,7,64,64]{3,2,1,0:T(8,128)} %multiply_add_fusion.2), channel_id=1, source_target_pairs={{0,8},{8,16},{16,24},{24,32},{32,40},{40,48},{48,56},{56,64},{64,7... | collective-permute-start | bytes 688136 | tf_op jit(solution)/shard_map/while/body/eval_jaxpr/ppermute | solution.py:12
  431.9 12.8 %collective-permute-start = (f32[2,7,64,64]{3,2,1,0:T(8,128)}, f32[2,7,64,64]{3,2,1,0:T(8,128)}, u32[]{:S(2)}, u32[]{:S(2)}) collective-permute-start(f32[2,7,64,64]{3,2,1,0:T(8,128)} %multiply_add_fusion.2), channel_id=1, source_target_pairs={{0,8},{8,16},{16,24},{24,32},{32,40},{40,48},{48,56},{56,64},{64,7... | collective-permute-start | bytes 688136 | tf_op jit(solution)/shard_map/while/body/eval_jaxpr/ppermute | solution.py:12
  446.8 13.4 %collective-permute-start = (f32[2,7,64,64]{3,2,1,0:T(8,128)}, f32[2,7,64,64]{3,2,1,0:T(8,128)}, u32[]{:S(2)}, u32[]{:S(2)}) collective-permute-start(f32[2,7,64,64]{3,2,1,0:T(8,128)} %multiply_add_fusion.2), channel_id=1, source_target_pairs={{0,8},{8,16},{16,24},{24,32},{32,40},{40,48},{48,56},{56,64},{64,7... | collective-permute-start | bytes 688136 | tf_op jit(solution)/shard_map/while/body/eval_jaxpr/ppermute | solution.py:12
  462.2 14.7 %collective-permute-start = (f32[2,7,64,64]{3,2,1,0:T(8,128)}, f32[2,7,64,64]{3,2,1,0:T(8,128)}, u32[]{:S(2)}, u32[]{:S(2)}) collective-permute-start(f32[2,7,64,64]{3,2,1,0:T(8,128)} %multiply_add_fusion.2), channel_id=1, source_target_pairs={{0,8},{8,16},{16,24},{24,32},{32,40},{40,48},{48,56},{56,64},{64,7... | collective-permute-start | bytes 688136 | tf_op jit(solution)/shard_map/while/body/eval_jaxpr/ppermute | solution.py:12
  479.0 16.4 %collective-permute-start = (f32[2,7,64,64]{3,2,1,0:T(8,128)}, f32[2,7,64,64]{3,2,1,0:T(8,128)}, u32[]{:S(2)}, u32[]{:S(2)}) collective-permute-start(f32[2,7,64,64]{3,2,1,0:T(8,128)} %multiply_add_fusion.2), channel_id=1, source_target_pairs={{0,8},{8,16},{16,24},{24,32},{32,40},{40,48},{48,56},{56,64},{64,7... | collective-permute-start | bytes 688136 | tf_op jit(solution)/shard_map/while/body/eval_jaxpr/ppermute | solution.py:12
  497.4 17.5 %collective-permute-start = (f32[2,7,64,64]{3,2,1,0:T(8,128)}, f32[2,7,64,64]{3,2,1,0:T(8,128)}, u32[]{:S(2)}, u32[]{:S(2)}) collective-permute-start(f32[2,7,64,64]{3,2,1,0:T(8,128)} %multiply_add_fusion.2), channel_id=1, source_target_pairs={{0,8},{8,16},{16,24},{24,32},{32,40},{40,48},{48,56},{56,64},{64,7... | collective-permute-start | bytes 688136 | tf_op jit(solution)/shard_map/while/body/eval_jaxpr/ppermute | solution.py:12
  517.0 18.5 %collective-permute-start = (f32[2,7,64,64]{3,2,1,0:T(8,128)}, f32[2,7,64,64]{3,2,1,0:T(8,128)}, u32[]{:S(2)}, u32[]{:S(2)}) collective-permute-start(f32[2,7,64,64]{3,2,1,0:T(8,128)} %multiply_add_fusion.2), channel_id=1, source_target_pairs={{0,8},{8,16},{16,24},{24,32},{32,40},{40,48},{48,56},{56,64},{64,7... | collective-permute-start | bytes 688136 | tf_op jit(solution)/shard_map/while/body/eval_jaxpr/ppermute | solution.py:12
  537.5 16.7 %collective-permute-start = (f32[2,7,64,64]{3,2,1,0:T(8,128)}, f32[2,7,64,64]{3,2,1,0:T(8,128)}, u32[]{:S(2)}, u32[]{:S(2)}) collective-permute-start(f32[2,7,64,64]{3,2,1,0:T(8,128)} %multiply_add_fusion.2), channel_id=1, source_target_pairs={{0,8},{8,16},{16,24},{24,32},{32,40},{40,48},{48,56},{56,64},{64,7... | collective-permute-start | bytes 688136 | tf_op jit(solution)/shard_map/while/body/eval_jaxpr/ppermute | solution.py:12
  556.3 15.0 %collective-permute-start = (f32[2,7,64,64]{3,2,1,0:T(8,128)}, f32[2,7,64,64]{3,2,1,0:T(8,128)}, u32[]{:S(2)}, u32[]{:S(2)}) collective-permute-start(f32[2,7,64,64]{3,2,1,0:T(8,128)} %multiply_add_fusion.2), channel_id=1, source_target_pairs={{0,8},{8,16},{16,24},{24,32},{32,40},{40,48},{48,56},{56,64},{64,7... | collective-permute-start | bytes 688136 | tf_op jit(solution)/shard_map/while/body/eval_jaxpr/ppermute | solution.py:12
  573.4 13.7 %collective-permute-start = (f32[2,7,64,64]{3,2,1,0:T(8,128)}, f32[2,7,64,64]{3,2,1,0:T(8,128)}, u32[]{:S(2)}, u32[]{:S(2)}) collective-permute-start(f32[2,7,64,64]{3,2,1,0:T(8,128)} %multiply_add_fusion.2), channel_id=1, source_target_pairs={{0,8},{8,16},{16,24},{24,32},{32,40},{40,48},{48,56},{56,64},{64,7... | collective-permute-start | bytes 688136 | tf_op jit(solution)/shard_map/while/body/eval_jaxpr/ppermute | solution.py:12
  589.1 12.8 %collective-permute-start = (f32[2,7,64,64]{3,2,1,0:T(8,128)}, f32[2,7,64,64]{3,2,1,0:T(8,128)}, u32[]{:S(2)}, u32[]{:S(2)}) collective-permute-start(f32[2,7,64,64]{3,2,1,0:T(8,128)} %multiply_add_fusion.2), channel_id=1, source_target_pairs={{0,8},{8,16},{16,24},{24,32},{32,40},{40,48},{48,56},{56,64},{64,7... | collective-permute-start | bytes 688136 | tf_op jit(solution)/shard_map/while/body/eval_jaxpr/ppermute | solution.py:12
  603.9 12.8 %collective-permute-start = (f32[2,7,64,64]{3,2,1,0:T(8,128)}, f32[2,7,64,64]{3,2,1,0:T(8,128)}, u32[]{:S(2)}, u32[]{:S(2)}) collective-permute-start(f32[2,7,64,64]{3,2,1,0:T(8,128)} %multiply_add_fusion.2), channel_id=1, source_target_pairs={{0,8},{8,16},{16,24},{24,32},{32,40},{40,48},{48,56},{56,64},{64,7... | collective-permute-start | bytes 688136 | tf_op jit(solution)/shard_map/while/body/eval_jaxpr/ppermute | solution.py:12
  620.4 0.8 copy-start.4
  621.2 5.3 copy-start.8
  623.3 3.0 copy-start.2
  631.1 88.5 %copy-start.9 = (f32[3584]{0:T(1024)S(1)}, f32[3584]{0:T(1024)}, u32[]{:S(2)}) copy-start(f32[3584]{0:T(1024)} %param.38) | copy-start | bytes 43012
  631.1 107.9 %copy-start.18 = (u32[256]{0:T(256)S(1)}, u32[256]{0:T(256)}, u32[]{:S(2)}) copy-start(u32[256]{0:T(256)} %constant.94) | copy-start | bytes 3076
  631.1 117.0 %copy-start.12 = (s32[256]{0:T(256)S(1)}, s32[256]{0:T(256)}, u32[]{:S(2)}) copy-start(s32[256]{0:T(256)} %param.21) | copy-start | bytes 3076
  634.7 215.0 %all-gather.5.cloned.1.call-start = ((), (), s32[]{:S(2)}) async-start(), calls=%async_computation.3 | async-start | bytes 15138816 | tf_op jit(solution)/shard_map/all_gather | solution.py:146
  720.7 9.1 collective-permute-start.1
  729.8 9.1 collective-permute-start.2
  729.8 9.8 collective-permute-start.5
  739.0 9.1 collective-permute-start.3
  739.6 10.1 collective-permute-start.6
  748.1 9.1 collective-permute-start.4
  749.7 13.1 %collective-permute-start.7 = (bf16[32,2,3584]{2,0,1:T(8,128)(2,1)S(1)}, bf16[32,2,3584]{2,0,1:T(8,128)(2,1)S(1)}, u32[]{:S(2)}, u32[]{:S(2)}) collective-permute-start(bf16[32,2,3584]{2,0,1:T(8,128)(2,1)S(1)} %collective-permute-done.6), channel_id=1, source_target_pairs={{0,7},{1,0},{2,1},{3,2},{4,3},{5,4},{6,5},{7,6},{8,15},{9,8},{10,9... | collective-permute-start | bytes 1376264 | tf_op jit(solution)/shard_map/ppermute | solution.py:139
  770.1 122.8 %copy-start.13 = (s32[256]{0:T(256)S(1)}, s32[256]{0:T(256)}, u32[]{:S(2)}) copy-start(s32[256]{0:T(256)} %param.22) | copy-start | bytes 3076
  770.1 122.8 %copy-start.16 = (s32[48]{0:T(128)S(1)}, s32[48]{0:T(128)}, u32[]{:S(2)}) copy-start(s32[48]{0:T(128)} %param.23) | copy-start | bytes 580
  770.1 122.9 %copy-start.17 = (s32[48]{0:T(128)S(1)}, s32[48]{0:T(128)}, u32[]{:S(2)}) copy-start(s32[48]{0:T(128)} %param.24) | copy-start | bytes 580
  849.7 183.9 %copy-start.1 = (bf16[448,3584]{1,0:T(8,128)(2,1)S(1)}, bf16[448,3584]{1,0:T(8,128)(2,1)}, u32[]{:S(2)}) copy-start(bf16[448,3584]{1,0:T(8,128)(2,1)} %param.34) | copy-start | bytes 9633796
  892.9 140.7 %copy-start.14 = (f32[256]{0:T(256)}, f32[256]{0:T(256)S(1)}, u32[]{:S(2)}) copy-start(f32[256]{0:T(256)S(1)} %convert_multiply_fusion.4) | copy-start | bytes 3076
Sparse Core Ops, SparseCore 0:
  10.6 94.5 all-gather.2
  634.9 83.3 reduce-scatter.1
  720.9 128.7 all-gather.4
